TPU v7x, 512 devices: a whole 4x8x8 slice. The times are simulated.
512 devices in a mesh: rows: 64 (over y, x, core), rhs: 8 (over z).
Axes of the slice: x: 4, y: 8, z: 8, core: 2. Of those that a mesh axis runs over, the one named last changes fastest.
Arguments:
- right_side: float32 [64, 32768], P('rhs', 'rows'), may hold values from -6 to 6
- tiles: float32 [512, 7, 64, 64], P('rows'), may hold values from -2 to 5.5, as said below
- pivots: float32 [512, 64, 64], P('rows'), may hold values from -0.05 to 0.8, as said below
- columns: int32 [512, 7], P('rows'), may hold values from 0 to 511, as said below
Outputs:
- solution: float32 [64, 32768], P('rhs', 'rows')
- residual: float32 [64, 32768], P('rhs', 'rows')
Inputs may be any that keep to these rules, and one draw needn't show every extreme that they name: columns[i, 0] = i. The other six columns of block row i are i - o and i + o for three offsets o shared by all block rows, the largest of them exactly 8, in an order of the slots drawn for each block row; a column that would fall outside 0 to 511 is i itself. tiles[i, 0] is the diagonal tile of block row i; A is symmetric positive definite: the tile of block row i in a slot whose column j differs from i is the transpose of the tile of block row j in its slot whose column is i. Every pivots[i] is symmetric positive definite.
All inputs are finite; a program needn't handle non-finite values.
Results may differ from a plain program's by a relative error of at most 0.0003.
Values sent between devices are 32-bit elements; how exact they have to be, the bound alone decides.
A program may use at most 64 MiB of HBM per device.

v0:
```python
import jax
import jax.numpy as jnp
from jax import lax
from jax.sharding import PartitionSpec as P

SPAN = 8
ITERS = 2


def passed_along(value, axis, steps):
    count = lax.axis_size(axis)
    first, last = (max(0, -steps), min(count, count - steps))
    return lax.ppermute(value, axis, [(source, source + steps) for source in range(first, last)])


def extended_2(block, sides, width):
    for axis, dim in sides:
        count = lax.axis_size(axis)
        forward = [(i, i + 1) for i in range(count - 1)]
        backward = [(target, source) for source, target in forward]
        low = lax.ppermute(
            lax.slice_in_dim(block, block.shape[dim] - width, None, axis=dim), axis, forward
        )
        high = lax.ppermute(lax.slice_in_dim(block, 0, width, axis=dim), axis, backward)
        block = jnp.concatenate([low, block, high], axis=dim)
    return block


def inner(left, right):
    return jnp.dot(left, right.T, precision=lax.Precision.HIGHEST)


def chol_solve(factor, values):
    middle = lax.linalg.triangular_solve(factor, values, left_side=True, lower=True)
    return lax.linalg.triangular_solve(factor, middle, left_side=True, lower=True, transpose_a=True)


def shards(right_side, tiles, pivots, columns):
    count = right_side.shape[0]
    shard_rows = tiles.shape[0]
    width = tiles.shape[2]
    cells = shard_rows * width
    where_row = lax.axis_index("rows")
    start = where_row * shard_rows
    position = where_row % SPAN
    block_low = (where_row - position) * shard_rows
    block_high = block_low + SPAN * shard_rows
    global_rows = start + jnp.arange(shard_rows, dtype=jnp.int32)
    lower = (columns < global_rows[:, None]) & (columns >= block_low)
    upper = (columns > global_rows[:, None]) & (columns < block_high)
    lower_tiles = tiles * lower[:, :, None, None].astype(tiles.dtype)
    upper_tiles = tiles * upper[:, :, None, None].astype(tiles.dtype)
    forward_cols = jnp.clip(columns - start + shard_rows, 0, 2 * shard_rows - 1)
    backward_cols = jnp.clip(columns - start, 0, 2 * shard_rows - 1)
    halo_cols = columns - start + shard_rows
    from_below = (position != 0).astype(jnp.float32)
    from_above = (position != SPAN - 1).astype(jnp.float32)

    def forward_local(source, incoming):
        extended = jnp.concatenate([incoming, jnp.zeros_like(source)], axis=1)

        def forward_one_row(row, extended):
            picked = jnp.take(extended, forward_cols[row], axis=1)
            summed = jnp.einsum(
                "kab,ckb->ca", lower_tiles[row], picked, precision=lax.Precision.HIGHEST
            )
            remain = source[:, row] - summed
            value = jnp.einsum("ab,cb->ca", pivots[row], remain, precision=lax.Precision.HIGHEST)
            return lax.dynamic_update_slice_in_dim(extended, value[:, None], shard_rows + row, 1)

        extended = lax.fori_loop(0, shard_rows, forward_one_row, extended)
        return extended[:, shard_rows:]

    def backward_local(source, incoming):
        extended = jnp.concatenate([jnp.zeros_like(source), incoming], axis=1)

        def backward_one_row(turn, extended):
            row = shard_rows - 1 - turn
            picked = jnp.take(extended, backward_cols[row], axis=1)
            summed = jnp.einsum(
                "kab,ckb->ca", upper_tiles[row], picked, precision=lax.Precision.HIGHEST
            )
            value = source[:, row] - jnp.einsum(
                "ab,cb->ca", pivots[row], summed, precision=lax.Precision.HIGHEST
            )
            return lax.dynamic_update_slice_in_dim(extended, value[:, None], row, 1)

        extended = lax.fori_loop(0, shard_rows, backward_one_row, extended)
        return extended[:, :shard_rows]

    def precondition(vector):
        source = vector.reshape(count, shard_rows, width)
        lowered = forward_local(source, jnp.zeros_like(source))
        for turn in range(SPAN - 1):
            incoming = passed_along(lowered, "rows", 1) * from_below
            lowered = forward_local(source, incoming)
        result = backward_local(lowered, jnp.zeros_like(lowered))
        for turn in range(SPAN - 1):
            incoming = passed_along(result, "rows", -1) * from_above
            result = backward_local(lowered, incoming)
        return result.reshape(count, cells)

    solution = jnp.zeros_like(right_side)
    residual = right_side
    direction = precondition(residual)
    for turn in range(ITERS):
        blocks = extended_2(direction, (("rows", 1),), cells).reshape(count, 3 * shard_rows, width)
        apply_picked = jnp.take(blocks, halo_cols, axis=1)
        image = jnp.einsum(
            "ikab,cikb->cia", tiles, apply_picked, precision=lax.Precision.HIGHEST
        ).reshape(count, cells)
        every_direction = lax.all_gather(direction, "rhs", axis=0, tiled=True)
        partial_pq = inner(every_direction, image)
        partial_pr = inner(every_direction, residual)
        summed_pq, summed_pr = lax.psum((partial_pq, partial_pr), "rows")
        gram = lax.all_gather(summed_pq, "rhs", axis=1, tiled=True)
        factor = jnp.linalg.cholesky(0.5 * (gram + gram.T))
        alpha = chol_solve(factor, summed_pr)
        change = jnp.dot(alpha.T, every_direction, precision=lax.Precision.HIGHEST)
        solution = solution + change
        if turn + 1 < ITERS:
            every_image = lax.all_gather(image, "rhs", axis=0, tiled=True)
            residual = residual - jnp.dot(alpha.T, every_image, precision=lax.Precision.HIGHEST)
            preconditioned = precondition(residual)
            summed_qz = lax.psum(inner(every_image, preconditioned), "rows")
            beta = -chol_solve(factor, summed_qz)
            direction = preconditioned + jnp.dot(
                beta.T, every_direction, precision=lax.Precision.HIGHEST
            )
        else:
            every_image = lax.all_gather(image, "rhs", axis=0, tiled=True)
            residual = residual - jnp.dot(alpha.T, every_image, precision=lax.Precision.HIGHEST)
    return (solution, residual)


def solution(mesh):
    return jax.shard_map(
        shards,
        mesh=mesh,
        in_specs=(
            P("rhs", "rows"),
            P("rows", None, None, None),
            P("rows", None, None),
            P("rows", None),
        ),
        out_specs=(P("rhs", "rows"), P("rhs", "rows")),
        check_vma=False,
    )
```

profile of v0, /device:TPU:32, one launch (start us, length us, event | category | flops | bytes accessed | tf_op | source)
XLA Modules:
  0.0 1239.9 jit_solution(11222102633937518841)
XLA Ops:
  6.0 16.7 %while.480 = (s32[]{:T(128)}, f32[8,16,64]{2,0,1:T(8,128)S(1)}, f32[8,8,64]{2,0,1:T(8,128)S(1)}, s32[8,7]{1,0:T(8,128)S(1)}, f32[8,7,64,64]{3,2,1,0:T(8,128)}, /...) while((s32[]{:T(128)}, f32[8,16,64]{2,0,1:T(8,128)S(1)}, ...), condition=%wide.region_1.3_spmd, body=%wide.region_0.2_spmd.sunk | while | flops 3150896 | bytes 322845 | solution.py:71
  31.3 16.7 %while.481 = (s32[]{:T(128)}, f32[8,16,64]{2,0,1:T(8,128)S(1)}, f32[8,8,64]{2,0,1:T(8,128)S(1)}, s32[8,7]{1,0:T(8,128)S(1)}, f32[8,7,64,64]{3,2,1,0:T(8,128)}, /...) while((s32[]{:T(128)}, f32[8,16,64]{2,0,1:T(8,128)S(1)}, ...), condition=%wide.region_3.5_spmd, body=%wide.region_2.4_spmd.sunk | while | flops 3150896 | bytes 322845 | solution.py:71
  56.6 16.7 %while.482 = (s32[]{:T(128)}, f32[8,16,64]{2,0,1:T(8,128)S(1)}, f32[8,8,64]{2,0,1:T(8,128)S(1)}, s32[8,7]{1,0:T(8,128)S(1)}, f32[8,7,64,64]{3,2,1,0:T(8,128)}, /...) while((s32[]{:T(128)}, f32[8,16,64]{2,0,1:T(8,128)S(1)}, ...), condition=%wide.region_5.7_spmd, body=%wide.region_4.6_spmd.sunk | while | flops 3150896 | bytes 322845 | solution.py:71
  81.9 16.7 %while.483 = (s32[]{:T(128)}, f32[8,16,64]{2,0,1:T(8,128)S(1)}, f32[8,8,64]{2,0,1:T(8,128)S(1)}, s32[8,7]{1,0:T(8,128)S(1)}, f32[8,7,64,64]{3,2,1,0:T(8,128)}, /...) while((s32[]{:T(128)}, f32[8,16,64]{2,0,1:T(8,128)S(1)}, ...), condition=%wide.region_7.9_spmd, body=%wide.region_6.8_spmd.sunk | while | flops 3150896 | bytes 322845 | solution.py:71
  107.2 16.7 %while.484 = (s32[]{:T(128)}, f32[8,16,64]{2,0,1:T(8,128)S(1)}, f32[8,8,64]{2,0,1:T(8,128)S(1)}, s32[8,7]{1,0:T(8,128)S(1)}, f32[8,7,64,64]{3,2,1,0:T(8,128)}, /...) while((s32[]{:T(128)}, f32[8,16,64]{2,0,1:T(8,128)S(1)}, ...), condition=%wide.region_9.11_spmd, body=%wide.region_8.10_spmd.sunk | while | flops 3150896 | bytes 322845 | solution.py:71
  132.5 16.7 %while.485 = (s32[]{:T(128)}, f32[8,16,64]{2,0,1:T(8,128)S(1)}, f32[8,8,64]{2,0,1:T(8,128)S(1)}, s32[8,7]{1,0:T(8,128)S(1)}, f32[8,7,64,64]{3,2,1,0:T(8,128)}, /...) while((s32[]{:T(128)}, f32[8,16,64]{2,0,1:T(8,128)S(1)}, ...), condition=%wide.region_11.13_spmd, body=%wide.region_10.12_spmd.sunk | while | flops 3150896 | bytes 322845 | solution.py:71
  157.8 16.7 %while.486 = (s32[]{:T(128)}, f32[8,16,64]{2,0,1:T(8,128)S(1)}, f32[8,8,64]{2,0,1:T(8,128)S(1)}, s32[8,7]{1,0:T(8,128)S(1)}, f32[8,7,64,64]{3,2,1,0:T(8,128)}, /...) while((s32[]{:T(128)}, f32[8,16,64]{2,0,1:T(8,128)S(1)}, ...), condition=%wide.region_13.15_spmd, body=%wide.region_12.14_spmd.sunk | while | flops 3150896 | bytes 322845 | solution.py:71
  183.1 16.7 %while.487 = (s32[]{:T(128)}, f32[8,16,64]{2,0,1:T(8,128)S(1)}, f32[8,8,64]{2,0,1:T(8,128)S(1)}, s32[8,7]{1,0:T(8,128)S(1)}, f32[8,7,64,64]{3,2,1,0:T(8,128)}, /...) while((s32[]{:T(128)}, f32[8,16,64]{2,0,1:T(8,128)S(1)}, ...), condition=%wide.region_15.17_spmd, body=%wide.region_14.16_spmd.sunk | while | flops 3150896 | bytes 322845 | solution.py:71
  199.9 9.2 while.488
  212.6 9.2 while.489
  221.8 7.0 collective-permute-start.8
  230.4 9.2 while.490
  239.6 7.0 collective-permute-start.9
  248.2 9.2 while.491
  257.4 7.0 collective-permute-start.10
  266.0 9.2 while.492
  275.2 7.0 collective-permute-start.11
  283.8 9.2 while.493
  293.0 7.0 collective-permute-start.12
  301.6 9.2 while.494
  319.4 9.2 while.495
  337.6 30.9 %all_gather.18 = f32[64,512]{1,0:T(8,128)S(1)} all-gather(f32[8,512]{1,0:T(8,128)S(1)} %reshape.66), channel_id=1, replica_groups=mesh['rows'=64,'rhs'=8] {'rhs'}, dimensions={0}, use_global_device_ids=true | all-gather | bytes 147456 | tf_op jit(solution)/shard_map/all_gather | solution.py:112
  373.2 24.6 %all_gather.20 = f32[64,512]{1,0:T(8,128)S(1)} all-gather(f32[8,512]{1,0:T(8,128)S(1)} %reshape.67), channel_id=1, replica_groups=mesh['rows'=64,'rhs'=8] {'rhs'}, dimensions={0}, use_global_device_ids=true | all-gather | bytes 147456 | tf_op jit(solution)/shard_map/all_gather | solution.py:122
  397.8 126.1 %all-reduce.29 = (f32[64,8]{0,1:T(8,128)S(1)}, f32[64,8]{0,1:T(8,128)S(1)}) all-reduce(f32[64,8]{0,1:T(8,128)S(1)} %fusion.476, f32[64,8]{0,1:T(8,128)S(1)} %fusion.475), channel_id=1, replica_groups=mesh['rows'=64,'rhs'=8] {'rows'}, use_global_device_ids=true, to_apply=%region_35.39 | all-reduce | flops 1024 | bytes 8192 | tf_op jit(solution)/shard_map/psum | solution.py:115
  523.9 24.5 %all_gather.19 = f32[64,64]{0,1:T(8,128)S(1)} all-gather(f32[64,8]{0,1:T(8,128)S(1)} %get-tuple-element.5610), channel_id=1, replica_groups=mesh['rows'=64,'rhs'=8] {'rhs'}, dimensions={1}, use_global_device_ids=true | all-gather | bytes 18432 | tf_op jit(solution)/shard_map/all_gather | solution.py:116
  561.3 16.7 %while.496 = (s32[]{:T(128)}, f32[8,16,64]{2,0,1:T(8,128)S(1)}, f32[8,8,64]{2,0,1:T(8,128)S(1)}, s32[8,7]{1,0:T(8,128)S(1)}, f32[8,7,64,64]{3,2,1,0:T(8,128)}, /...) while((s32[]{:T(128)}, f32[8,16,64]{2,0,1:T(8,128)S(1)}, ...), condition=%wide.region_37.43_spmd, body=%wide.region_36.42_spmd.sunk | while | flops 3150896 | bytes 322845 | solution.py:71
  586.6 16.7 %while.497 = (s32[]{:T(128)}, f32[8,16,64]{2,0,1:T(8,128)S(1)}, f32[8,8,64]{2,0,1:T(8,128)S(1)}, s32[8,7]{1,0:T(8,128)S(1)}, f32[8,7,64,64]{3,2,1,0:T(8,128)}, /...) while((s32[]{:T(128)}, f32[8,16,64]{2,0,1:T(8,128)S(1)}, ...), condition=%wide.region_39.45_spmd, body=%wide.region_38.44_spmd.sunk | while | flops 3150896 | bytes 322845 | solution.py:71
  611.9 16.7 %while.498 = (s32[]{:T(128)}, f32[8,16,64]{2,0,1:T(8,128)S(1)}, f32[8,8,64]{2,0,1:T(8,128)S(1)}, s32[8,7]{1,0:T(8,128)S(1)}, f32[8,7,64,64]{3,2,1,0:T(8,128)}, /...) while((s32[]{:T(128)}, f32[8,16,64]{2,0,1:T(8,128)S(1)}, ...), condition=%wide.region_41.47_spmd, body=%wide.region_40.46_spmd.sunk | while | flops 3150896 | bytes 322845 | solution.py:71
  637.2 16.7 %while.499 = (s32[]{:T(128)}, f32[8,16,64]{2,0,1:T(8,128)S(1)}, f32[8,8,64]{2,0,1:T(8,128)S(1)}, s32[8,7]{1,0:T(8,128)S(1)}, f32[8,7,64,64]{3,2,1,0:T(8,128)}, /...) while((s32[]{:T(128)}, f32[8,16,64]{2,0,1:T(8,128)S(1)}, ...), condition=%wide.region_43.49_spmd, body=%wide.region_42.48_spmd.sunk | while | flops 3150896 | bytes 322845 | solution.py:71
  662.5 16.7 %while.500 = (s32[]{:T(128)}, f32[8,16,64]{2,0,1:T(8,128)S(1)}, f32[8,8,64]{2,0,1:T(8,128)S(1)}, s32[8,7]{1,0:T(8,128)S(1)}, f32[8,7,64,64]{3,2,1,0:T(8,128)}, /...) while((s32[]{:T(128)}, f32[8,16,64]{2,0,1:T(8,128)S(1)}, ...), condition=%wide.region_45.51_spmd, body=%wide.region_44.50_spmd.sunk | while | flops 3150896 | bytes 322845 | solution.py:71
  687.8 16.7 %while.501 = (s32[]{:T(128)}, f32[8,16,64]{2,0,1:T(8,128)S(1)}, f32[8,8,64]{2,0,1:T(8,128)S(1)}, s32[8,7]{1,0:T(8,128)S(1)}, f32[8,7,64,64]{3,2,1,0:T(8,128)}, /...) while((s32[]{:T(128)}, f32[8,16,64]{2,0,1:T(8,128)S(1)}, ...), condition=%wide.region_47.53_spmd, body=%wide.region_46.52_spmd.sunk | while | flops 3150896 | bytes 322845 | solution.py:71
  713.1 16.7 %while.502 = (s32[]{:T(128)}, f32[8,16,64]{2,0,1:T(8,128)S(1)}, f32[8,8,64]{2,0,1:T(8,128)S(1)}, s32[8,7]{1,0:T(8,128)S(1)}, f32[8,7,64,64]{3,2,1,0:T(8,128)}, /...) while((s32[]{:T(128)}, f32[8,16,64]{2,0,1:T(8,128)S(1)}, ...), condition=%wide.region_49.55_spmd, body=%wide.region_48.54_spmd.sunk | while | flops 3150896 | bytes 322845 | solution.py:71
  738.4 16.7 %while.503 = (s32[]{:T(128)}, f32[8,16,64]{2,0,1:T(8,128)S(1)}, f32[8,8,64]{2,0,1:T(8,128)S(1)}, s32[8,7]{1,0:T(8,128)S(1)}, f32[8,7,64,64]{3,2,1,0:T(8,128)}, /...) while((s32[]{:T(128)}, f32[8,16,64]{2,0,1:T(8,128)S(1)}, ...), condition=%wide.region_51.57_spmd, body=%wide.region_50.56_spmd.sunk | while | flops 3150896 | bytes 322845 | solution.py:71
  755.2 9.2 while.504
  767.9 9.2 while.505
  785.7 9.2 while.506
  794.9 7.0 collective-permute-start.25
  803.5 9.2 while.507
  821.3 9.2 while.508
  839.1 9.2 while.509
  848.3 7.0 collective-permute-start.28
  856.9 9.2 while.510
  874.7 9.2 while.511
  884.2 129.3 %psum.37 = f32[64,8]{0,1:T(8,128)S(1)} all-reduce(f32[64,8]{0,1:T(8,128)S(1)} %fusion.478), channel_id=1, replica_groups=mesh['rows'=64,'rhs'=8] {'rows'}, use_global_device_ids=true, to_apply=%region_68.74 | all-reduce | flops 512 | bytes 4096 | tf_op jit(solution)/shard_map/psum | solution.py:125
  1022.8 24.6 %all_gather.21 = f32[64,512]{1,0:T(8,128)S(1)} all-gather(f32[8,512]{1,0:T(8,128)S(1)} %convolution_add_fusion.1), channel_id=1, replica_groups=mesh['rows'=64,'rhs'=8] {'rhs'}, dimensions={0}, use_global_device_ids=true | all-gather | bytes 147456 | tf_op jit(solution)/shard_map/all_gather | solution.py:112
  1050.5 24.6 %all_gather.23 = f32[64,512]{1,0:T(8,128)S(1)} all-gather(f32[8,512]{1,0:T(8,128)S(1)} %reshape.71), channel_id=1, replica_groups=mesh['rows'=64,'rhs'=8] {'rhs'}, dimensions={0}, use_global_device_ids=true | all-gather | bytes 147456 | tf_op jit(solution)/shard_map/all_gather | solution.py:131
  1075.2 126.1 %all-reduce.28 = (f32[64,8]{0,1:T(8,128)S(1)}, f32[64,8]{0,1:T(8,128)S(1)}) all-reduce(f32[64,8]{0,1:T(8,128)S(1)} %fusion.480, f32[64,8]{0,1:T(8,128)S(1)} %fusion.479), channel_id=1, replica_groups=mesh['rows'=64,'rhs'=8] {'rows'}, use_global_device_ids=true, to_apply=%region_70.76 | all-reduce | flops 1024 | bytes 8192 | tf_op jit(solution)/shard_map/psum | solution.py:115
  1201.3 24.5 %all_gather.22 = f32[64,64]{0,1:T(8,128)S(1)} all-gather(f32[64,8]{0,1:T(8,128)S(1)} %get-tuple-element.5608), channel_id=1, replica_groups=mesh['rows'=64,'rhs'=8] {'rhs'}, dimensions={1}, use_global_device_ids=true | all-gather | bytes 18432 | tf_op jit(solution)/shard_map/all_gather | solution.py:116
  (1499 shorter events, 647.7 us)
Async XLA Ops:
  2.9 3.1 copy-start
  22.7 8.6 collective-permute-start
  48.0 8.6 collective-permute-start.1
  73.3 8.6 collective-permute-start.2
  98.6 8.6 collective-permute-start.3
  123.9 8.6 collective-permute-start.4
  149.2 8.6 collective-permute-start.5
  174.5 8.6 collective-permute-start.6
  209.1 3.5 collective-permute-start.7
  221.8 8.6 collective-permute-start.8
  239.6 8.6 collective-permute-start.9
  257.4 8.6 collective-permute-start.10
  275.2 8.6 collective-permute-start.11
  293.0 8.6 collective-permute-start.12
  310.8 57.8 %copy-start.2 = (f32[8,512]{1,0:T(8,128)S(1)}, f32[8,512]{1,0:T(8,128)}, u32[]{:S(2)}) copy-start(f32[8,512]{1,0:T(8,128)} %param.77) | copy-start | bytes 49156
  310.8 8.6 collective-permute-start.13
  328.7 40.0 %collective-permute-start.14 = (f32[8,512]{1,0:T(8,128)S(1)}, f32[8,512]{1,0:T(8,128)S(1)}, u32[]{:S(2)}, u32[]{:S(2)}) collective-permute-start(f32[8,512]{1,0:T(8,128)S(1)} %reshape.66), channel_id=1, source_target_pairs={{0,8},{8,16},{16,24},{24,32},{32,40},{40,48},{48,56},{56,64},{64,7... | collective-permute-start | bytes 49160 | tf_op jit(solution)/shard_map/ppermute | solution.py:21
  330.6 38.2 %collective-permute-start.15 = (f32[8,512]{1,0:T(8,128)S(1)}, f32[8,512]{1,0:T(8,128)S(1)}, u32[]{:S(2)}, u32[]{:S(2)}) collective-permute-start(f32[8,512]{1,0:T(8,128)S(1)} %reshape.66), channel_id=1, source_target_pairs={{8,0},{16,8},{24,16},{32,24},{40,32},{48,40},{56,48},{64,56},{72,6... | collective-permute-start | bytes 49160 | tf_op jit(solution)/shard_map/ppermute | solution.py:24
  578.0 8.6 collective-permute-start.16
  603.3 8.6 collective-permute-start.17
  628.6 8.6 collective-permute-start.18
  653.9 8.6 collective-permute-start.19
  679.2 8.6 collective-permute-start.20
  704.5 8.6 collective-permute-start.21
  729.8 8.6 collective-permute-start.22
  764.4 3.5 collective-permute-start.23
  777.1 8.6 collective-permute-start.24
  794.9 8.6 collective-permute-start.25
  812.7 8.6 collective-permute-start.26
  830.5 8.6 collective-permute-start.27
  848.3 8.6 collective-permute-start.28
  866.1 8.6 collective-permute-start.29
  883.9 164.5 %copy-start.1 = (f32[8,7,64,64]{3,2,1,0:T(8,128)S(1)}, f32[8,7,64,64]{3,2,1,0:T(8,128)}, u32[]{:S(2)}) copy-start(f32[8,7,64,64]{3,2,1,0:T(8,128)} %param.78) | copy-start | bytes 2752516
  1013.9 33.6 %collective-permute-start.30 = (f32[8,512]{1,0:T(8,128)S(1)}, f32[8,512]{1,0:T(8,128)S(1)}, u32[]{:S(2)}, u32[]{:S(2)}) collective-permute-start(f32[8,512]{1,0:T(8,128)S(1)} %convolution_add_fusion.1), channel_id=1, source_target_pairs={{0,8},{8,16},{16,24},{24,32},{32,40},{40,48},{48,56},{56,64},{64,7... | collective-permute-start | bytes 49160 | tf_op jit(solution)/shard_map/ppermute | solution.py:21
  1015.9 31.8 %collective-permute-start.31 = (f32[8,512]{1,0:T(8,128)S(1)}, f32[8,512]{1,0:T(8,128)S(1)}, u32[]{:S(2)}, u32[]{:S(2)}) collective-permute-start(f32[8,512]{1,0:T(8,128)S(1)} %convolution_add_fusion.1), channel_id=1, source_target_pairs={{8,0},{16,8},{24,16},{32,24},{40,32},{48,40},{56,48},{64,56},{72,6... | collective-permute-start | bytes 49160 | tf_op jit(solution)/shard_map/ppermute | solution.py:24
where the time goes:
time: 1240 us
  blocking collectives  535 us (43%)
  matrix products  265 us (21%)
  local copies, waits for them, and re-layouts  146 us (12%)
  starting transfers between devices  133 us (11%)
  waiting for transfers between devices  114 us (9%)
  other arithmetic  39.3 us (3%)
    psum x2, blocking collectives, shards(): summed_pq, summed_pr = lax.psum((partial_pq, partial_pr), 'rows')  252 us
    dot_general x128, matrix products, forward_one_row(): jnp.einsum('kab,ckb->ca', lower_tiles[row], picked, precision=lax.Precisi...  162 us
    psum x1, blocking collectives, shards(): summed_qz = lax.psum(inner(every_image, preconditioned), 'rows')  129 us
    ppermute x28, starting transfers between devices, passed_along(): lax.ppermute(value, axis, [(source, source + steps) for source in range(f...  115 us
    ppermute x28, waiting for transfers between devices, passed_along(): lax.ppermute(value, axis, [(source, source + steps) for source in range(f...  114 us
    gather x128, local copies, waits for them, and re-layouts, forward_one_row(): picked = jnp.take(extended, forward_cols[row], axis=1)  70.9 us
    gather x128, local copies, waits for them, and re-layouts, backward_one_row(): picked = jnp.take(extended, backward_cols[row], axis=1)  70.9 us
    all_gather x2, blocking collectives, shards(): every_direction = lax.all_gather(direction, 'rhs', axis=0, tiled=True)  55.5 us
  transfers between devices with their start and end apart: 32, of which 28 were waited for; matrix products, arithmetic and copies ran while one was open for 0% of the time, Pallas kernels for 0%

commit v1 on v0

--- a/solution.py
+++ b/solution.py
@@ -2,6 +2,7 @@
 import jax.numpy as jnp
 from jax import lax
 from jax.sharding import PartitionSpec as P
+from jax.lax import all_to_all, axis_size
 
 SPAN = 8
 ITERS = 2
@@ -109,7 +110,9 @@
         image = jnp.einsum(
             "ikab,cikb->cia", tiles, apply_picked, precision=lax.Precision.HIGHEST
         ).reshape(count, cells)
-        every_direction = lax.all_gather(direction, "rhs", axis=0, tiled=True)
+        every_direction = jnp.concatenate(
+            all_to_all(jnp.stack(axis_size("rhs") * [direction], axis=0), "rhs", 0, 0), 0
+        )
         partial_pq = inner(every_direction, image)
         partial_pr = inner(every_direction, residual)
         summed_pq, summed_pr = lax.psum((partial_pq, partial_pr), "rows")

time: 1240 us -> 1210 us (0.976)
  blocking collectives: 535 us -> 483 us
  starting transfers between devices: 133 us -> 149 us
    all_gather x2 -> x0, blocking collectives: 55.5 us -> none  [shards(): every_direction = lax.all_gather(direction, 'rhs', axis=0, tiled=True)]
    all_to_all x0 -> x2, starting transfers between devices: none -> 16.2 us  [shards(): all_to_all(jnp.stack(axis_size('rhs') * [direction], axis=0), 'rhs', 0, 0)]
  transfers between devices with their start and end apart: 32 -> 34, of which waited for: 28 -> 28; matrix products, arithmetic and copies ran while one was open for 0% -> 1% of each run, Pallas kernels for 0% -> 0%
where the time goes in v1:
time: 1210 us
  blocking collectives  483 us (40%)
  matrix products  265 us (22%)
  starting transfers between devices  149 us (12%)
  local copies, waits for them, and re-layouts  147 us (12%)
  waiting for transfers between devices  115 us (10%)
  other arithmetic  39.2 us (3%)
    psum x2, blocking collectives, shards(): summed_pq, summed_pr = lax.psum((partial_pq, partial_pr), 'rows')  252 us
    dot_general x128, matrix products, forward_one_row(): jnp.einsum('kab,ckb->ca', lower_tiles[row], picked, precision=lax.Precisi...  162 us
    psum x1, blocking collectives, shards(): summed_qz = lax.psum(inner(every_image, preconditioned), 'rows')  129 us
    ppermute x28, starting transfers between devices, passed_along(): lax.ppermute(value, axis, [(source, source + steps) for source in range(f...  115 us
    ppermute x28, waiting for transfers between devices, passed_along(): lax.ppermute(value, axis, [(source, source + steps) for source in range(f...  115 us
    gather x128, local copies, waits for them, and re-layouts, forward_one_row(): picked = jnp.take(extended, forward_cols[row], axis=1)  70.9 us
    gather x128, local copies, waits for them, and re-layouts, backward_one_row(): picked = jnp.take(extended, backward_cols[row], axis=1)  70.9 us
    all_gather x2, blocking collectives, shards(): every_image = lax.all_gather(image, 'rhs', axis=0, tiled=True)  52.1 us
  transfers between devices with their start and end apart: 34, of which 28 were waited for; matrix products, arithmetic and copies ran while one was open for 1% of the time, Pallas kernels for 0%

profile of v1, /device:TPU:32, one launch (start us, length us, event | category | flops | bytes accessed | tf_op | source)
XLA Modules:
  0.0 1205.0 jit_solution(1830713024037099838)
XLA Ops:
  6.0 16.7 %while.480 = (s32[]{:T(128)}, f32[8,16,64]{2,0,1:T(8,128)S(1)}, f32[8,8,64]{2,0,1:T(8,128)S(1)}, s32[8,7]{1,0:T(8,128)S(1)}, f32[8,7,64,64]{3,2,1,0:T(8,128)}, /...) while((s32[]{:T(128)}, f32[8,16,64]{2,0,1:T(8,128)S(1)}, ...), condition=%wide.region_1.3_spmd, body=%wide.region_0.2_spmd.sunk | while | flops 3150896 | bytes 322845 | solution.py:72
  31.3 16.7 %while.481 = (s32[]{:T(128)}, f32[8,16,64]{2,0,1:T(8,128)S(1)}, f32[8,8,64]{2,0,1:T(8,128)S(1)}, s32[8,7]{1,0:T(8,128)S(1)}, f32[8,7,64,64]{3,2,1,0:T(8,128)}, /...) while((s32[]{:T(128)}, f32[8,16,64]{2,0,1:T(8,128)S(1)}, ...), condition=%wide.region_3.5_spmd, body=%wide.region_2.4_spmd.sunk | while | flops 3150896 | bytes 322845 | solution.py:72
  56.6 16.7 %while.482 = (s32[]{:T(128)}, f32[8,16,64]{2,0,1:T(8,128)S(1)}, f32[8,8,64]{2,0,1:T(8,128)S(1)}, s32[8,7]{1,0:T(8,128)S(1)}, f32[8,7,64,64]{3,2,1,0:T(8,128)}, /...) while((s32[]{:T(128)}, f32[8,16,64]{2,0,1:T(8,128)S(1)}, ...), condition=%wide.region_5.7_spmd, body=%wide.region_4.6_spmd.sunk | while | flops 3150896 | bytes 322845 | solution.py:72
  81.9 16.7 %while.483 = (s32[]{:T(128)}, f32[8,16,64]{2,0,1:T(8,128)S(1)}, f32[8,8,64]{2,0,1:T(8,128)S(1)}, s32[8,7]{1,0:T(8,128)S(1)}, f32[8,7,64,64]{3,2,1,0:T(8,128)}, /...) while((s32[]{:T(128)}, f32[8,16,64]{2,0,1:T(8,128)S(1)}, ...), condition=%wide.region_7.9_spmd, body=%wide.region_6.8_spmd.sunk | while | flops 3150896 | bytes 322845 | solution.py:72
  107.2 16.7 %while.484 = (s32[]{:T(128)}, f32[8,16,64]{2,0,1:T(8,128)S(1)}, f32[8,8,64]{2,0,1:T(8,128)S(1)}, s32[8,7]{1,0:T(8,128)S(1)}, f32[8,7,64,64]{3,2,1,0:T(8,128)}, /...) while((s32[]{:T(128)}, f32[8,16,64]{2,0,1:T(8,128)S(1)}, ...), condition=%wide.region_9.11_spmd, body=%wide.region_8.10_spmd.sunk | while | flops 3150896 | bytes 322845 | solution.py:72
  132.5 16.7 %while.485 = (s32[]{:T(128)}, f32[8,16,64]{2,0,1:T(8,128)S(1)}, f32[8,8,64]{2,0,1:T(8,128)S(1)}, s32[8,7]{1,0:T(8,128)S(1)}, f32[8,7,64,64]{3,2,1,0:T(8,128)}, /...) while((s32[]{:T(128)}, f32[8,16,64]{2,0,1:T(8,128)S(1)}, ...), condition=%wide.region_11.13_spmd, body=%wide.region_10.12_spmd.sunk | while | flops 3150896 | bytes 322845 | solution.py:72
  157.8 16.7 %while.486 = (s32[]{:T(128)}, f32[8,16,64]{2,0,1:T(8,128)S(1)}, f32[8,8,64]{2,0,1:T(8,128)S(1)}, s32[8,7]{1,0:T(8,128)S(1)}, f32[8,7,64,64]{3,2,1,0:T(8,128)}, /...) while((s32[]{:T(128)}, f32[8,16,64]{2,0,1:T(8,128)S(1)}, ...), condition=%wide.region_13.15_spmd, body=%wide.region_12.14_spmd.sunk | while | flops 3150896 | bytes 322845 | solution.py:72
  183.1 16.7 %while.487 = (s32[]{:T(128)}, f32[8,16,64]{2,0,1:T(8,128)S(1)}, f32[8,8,64]{2,0,1:T(8,128)S(1)}, s32[8,7]{1,0:T(8,128)S(1)}, f32[8,7,64,64]{3,2,1,0:T(8,128)}, /...) while((s32[]{:T(128)}, f32[8,16,64]{2,0,1:T(8,128)S(1)}, ...), condition=%wide.region_15.17_spmd, body=%wide.region_14.16_spmd.sunk | while | flops 3150896 | bytes 322845 | solution.py:72
  199.9 9.2 while.488
  212.6 9.2 while.489
  221.8 7.0 collective-permute-start.8
  230.4 9.2 while.490
  239.6 7.0 collective-permute-start.9
  248.2 9.2 while.491
  257.4 7.0 collective-permute-start.10
  266.0 9.2 while.492
  275.2 7.0 collective-permute-start.11
  283.8 9.2 while.493
  293.0 7.0 collective-permute-start.12
  301.6 9.2 while.494
  319.4 9.2 while.495
  338.3 10.4 all-to-all-start
  353.0 26.0 %all_gather.13 = f32[64,512]{1,0:T(8,128)S(1)} all-gather(f32[8,512]{1,0:T(8,128)S(1)} %reshape.75), channel_id=1, replica_groups=mesh['rows'=64,'rhs'=8] {'rhs'}, dimensions={0}, use_global_device_ids=true | all-gather | bytes 147456 | tf_op jit(solution)/shard_map/all_gather | solution.py:125
  379.4 126.1 %all-reduce.29 = (f32[64,8]{0,1:T(8,128)S(1)}, f32[64,8]{0,1:T(8,128)S(1)}) all-reduce(f32[64,8]{0,1:T(8,128)S(1)} %fusion.460, f32[64,8]{0,1:T(8,128)S(1)} %fusion.462), channel_id=1, replica_groups=mesh['rows'=64,'rhs'=8] {'rows'}, use_global_device_ids=true, to_apply=%region_35.39 | all-reduce | flops 1024 | bytes 8192 | tf_op jit(solution)/shard_map/psum | solution.py:118
  505.6 24.5 %all_gather.12 = f32[64,64]{0,1:T(8,128)S(1)} all-gather(f32[64,8]{0,1:T(8,128)S(1)} %get-tuple-element.5610), channel_id=1, replica_groups=mesh['rows'=64,'rhs'=8] {'rhs'}, dimensions={1}, use_global_device_ids=true | all-gather | bytes 18432 | tf_op jit(solution)/shard_map/all_gather | solution.py:119
  543.0 16.7 %while.496 = (s32[]{:T(128)}, f32[8,16,64]{2,0,1:T(8,128)S(1)}, f32[8,8,64]{2,0,1:T(8,128)S(1)}, s32[8,7]{1,0:T(8,128)S(1)}, f32[8,7,64,64]{3,2,1,0:T(8,128)}, /...) while((s32[]{:T(128)}, f32[8,16,64]{2,0,1:T(8,128)S(1)}, ...), condition=%wide.region_37.43_spmd, body=%wide.region_36.42_spmd.sunk | while | flops 3150896 | bytes 322845 | solution.py:72
  568.3 16.7 %while.497 = (s32[]{:T(128)}, f32[8,16,64]{2,0,1:T(8,128)S(1)}, f32[8,8,64]{2,0,1:T(8,128)S(1)}, s32[8,7]{1,0:T(8,128)S(1)}, f32[8,7,64,64]{3,2,1,0:T(8,128)}, /...) while((s32[]{:T(128)}, f32[8,16,64]{2,0,1:T(8,128)S(1)}, ...), condition=%wide.region_39.45_spmd, body=%wide.region_38.44_spmd.sunk | while | flops 3150896 | bytes 322845 | solution.py:72
  593.6 16.7 %while.498 = (s32[]{:T(128)}, f32[8,16,64]{2,0,1:T(8,128)S(1)}, f32[8,8,64]{2,0,1:T(8,128)S(1)}, s32[8,7]{1,0:T(8,128)S(1)}, f32[8,7,64,64]{3,2,1,0:T(8,128)}, /...) while((s32[]{:T(128)}, f32[8,16,64]{2,0,1:T(8,128)S(1)}, ...), condition=%wide.region_41.47_spmd, body=%wide.region_40.46_spmd.sunk | while | flops 3150896 | bytes 322845 | solution.py:72
  618.9 16.7 %while.499 = (s32[]{:T(128)}, f32[8,16,64]{2,0,1:T(8,128)S(1)}, f32[8,8,64]{2,0,1:T(8,128)S(1)}, s32[8,7]{1,0:T(8,128)S(1)}, f32[8,7,64,64]{3,2,1,0:T(8,128)}, /...) while((s32[]{:T(128)}, f32[8,16,64]{2,0,1:T(8,128)S(1)}, ...), condition=%wide.region_43.49_spmd, body=%wide.region_42.48_spmd.sunk | while | flops 3150896 | bytes 322845 | solution.py:72
  644.2 16.7 %while.500 = (s32[]{:T(128)}, f32[8,16,64]{2,0,1:T(8,128)S(1)}, f32[8,8,64]{2,0,1:T(8,128)S(1)}, s32[8,7]{1,0:T(8,128)S(1)}, f32[8,7,64,64]{3,2,1,0:T(8,128)}, /...) while((s32[]{:T(128)}, f32[8,16,64]{2,0,1:T(8,128)S(1)}, ...), condition=%wide.region_45.51_spmd, body=%wide.region_44.50_spmd.sunk | while | flops 3150896 | bytes 322845 | solution.py:72
  669.5 16.7 %while.501 = (s32[]{:T(128)}, f32[8,16,64]{2,0,1:T(8,128)S(1)}, f32[8,8,64]{2,0,1:T(8,128)S(1)}, s32[8,7]{1,0:T(8,128)S(1)}, f32[8,7,64,64]{3,2,1,0:T(8,128)}, /...) while((s32[]{:T(128)}, f32[8,16,64]{2,0,1:T(8,128)S(1)}, ...), condition=%wide.region_47.53_spmd, body=%wide.region_46.52_spmd.sunk | while | flops 3150896 | bytes 322845 | solution.py:72
  694.8 16.7 %while.502 = (s32[]{:T(128)}, f32[8,16,64]{2,0,1:T(8,128)S(1)}, f32[8,8,64]{2,0,1:T(8,128)S(1)}, s32[8,7]{1,0:T(8,128)S(1)}, f32[8,7,64,64]{3,2,1,0:T(8,128)}, /...) while((s32[]{:T(128)}, f32[8,16,64]{2,0,1:T(8,128)S(1)}, ...), condition=%wide.region_49.55_spmd, body=%wide.region_48.54_spmd.sunk | while | flops 3150896 | bytes 322845 | solution.py:72
  720.1 16.7 %while.503 = (s32[]{:T(128)}, f32[8,16,64]{2,0,1:T(8,128)S(1)}, f32[8,8,64]{2,0,1:T(8,128)S(1)}, s32[8,7]{1,0:T(8,128)S(1)}, f32[8,7,64,64]{3,2,1,0:T(8,128)}, /...) while((s32[]{:T(128)}, f32[8,16,64]{2,0,1:T(8,128)S(1)}, ...), condition=%wide.region_51.57_spmd, body=%wide.region_50.56_spmd.sunk | while | flops 3150896 | bytes 322845 | solution.py:72
  736.8 9.2 while.504
  749.6 9.2 while.505
  767.4 9.2 while.506
  776.6 7.0 collective-permute-start.25
  785.2 9.2 while.507
  802.9 9.2 while.508
  812.2 7.0 collective-permute-start.27
  820.7 9.2 while.509
  838.5 9.2 while.510
  847.7 7.0 collective-permute-start.29
  856.3 9.2 while.511
  865.8 129.3 %psum.37 = f32[64,8]{0,1:T(8,128)S(1)} all-reduce(f32[64,8]{0,1:T(8,128)S(1)} %fusion.487), channel_id=1, replica_groups=mesh['rows'=64,'rhs'=8] {'rows'}, use_global_device_ids=true, to_apply=%region_68.74 | all-reduce | flops 512 | bytes 4096 | tf_op jit(solution)/shard_map/psum | solution.py:128
  1013.8 26.0 %all_gather.15 = f32[64,512]{1,0:T(8,128)S(1)} all-gather(f32[8,512]{1,0:T(8,128)S(1)} %reshape.80), channel_id=1, replica_groups=mesh['rows'=64,'rhs'=8] {'rhs'}, dimensions={0}, use_global_device_ids=true | all-gather | bytes 147456 | tf_op jit(solution)/shard_map/all_gather | solution.py:134
  1040.2 126.1 %all-reduce.28 = (f32[64,8]{0,1:T(8,128)S(1)}, f32[64,8]{0,1:T(8,128)S(1)}) all-reduce(f32[64,8]{0,1:T(8,128)S(1)} %fusion.453, f32[64,8]{0,1:T(8,128)S(1)} %fusion.455), channel_id=1, replica_groups=mesh['rows'=64,'rhs'=8] {'rows'}, use_global_device_ids=true, to_apply=%region_70.76 | all-reduce | flops 1024 | bytes 8192 | tf_op jit(solution)/shard_map/psum | solution.py:118
  1166.4 24.5 %all_gather.14 = f32[64,64]{0,1:T(8,128)S(1)} all-gather(f32[64,8]{0,1:T(8,128)S(1)} %get-tuple-element.5608), channel_id=1, replica_groups=mesh['rows'=64,'rhs'=8] {'rhs'}, dimensions={1}, use_global_device_ids=true | all-gather | bytes 18432 | tf_op jit(solution)/shard_map/all_gather | solution.py:119
  (1503 shorter events, 648.0 us)
Async XLA Ops:
  2.9 3.1 copy-start
  22.7 8.6 collective-permute-start
  48.0 8.6 collective-permute-start.1
  73.3 8.6 collective-permute-start.2
  98.6 8.6 collective-permute-start.3
  123.9 8.6 collective-permute-start.4
  149.2 8.6 collective-permute-start.5
  174.5 8.6 collective-permute-start.6
  209.1 3.5 collective-permute-start.7
  221.8 8.6 collective-permute-start.8
  239.6 8.6 collective-permute-start.9
  257.4 8.6 collective-permute-start.10
  275.2 8.6 collective-permute-start.11
  293.0 8.6 collective-permute-start.12
  310.8 8.6 collective-permute-start.13
  328.7 20.0 %collective-permute-start.14 = (f32[8,512]{1,0:T(8,128)S(1)}, f32[8,512]{1,0:T(8,128)S(1)}, u32[]{:S(2)}, u32[]{:S(2)}) collective-permute-start(f32[8,512]{1,0:T(8,128)S(1)} %stack_reshape.2), channel_id=1, source_target_pairs={{0,8},{8,16},{16,24},{24,32},{32,40},{40,48},{48,56},{56,64},{64,7... | collective-permute-start | bytes 49160 | tf_op jit(solution)/shard_map/ppermute | solution.py:22
  330.6 18.2 %collective-permute-start.15 = (f32[8,512]{1,0:T(8,128)S(1)}, f32[8,512]{1,0:T(8,128)S(1)}, u32[]{:S(2)}, u32[]{:S(2)}) collective-permute-start(f32[8,512]{1,0:T(8,128)S(1)} %stack_reshape.2), channel_id=1, source_target_pairs={{8,0},{16,8},{24,16},{32,24},{40,32},{48,40},{56,48},{64,56},{72,6... | collective-permute-start | bytes 49160 | tf_op jit(solution)/shard_map/ppermute | solution.py:25
  338.3 41.0 %copy-start.2 = (f32[8,512]{1,0:T(8,128)S(1)}, f32[8,512]{1,0:T(8,128)}, u32[]{:S(2)}) copy-start(f32[8,512]{1,0:T(8,128)} %param.77) | copy-start | bytes 49156
  338.3 40.8 %all-to-all-start = ((f32[8,8,512]{2,1,0:T(8,128)}), f32[8,8,512]{2,1,0:T(8,128)S(1)}, u32[]{:S(2)}, u32[]{:S(2)}) async-start(f32[8,8,512]{2,1,0:T(8,128)} %stack.4), calls=%async_computation | async-start | bytes 262144 | tf_op jit(solution)/shard_map/all_to_all | solution.py:114
  559.7 8.6 collective-permute-start.16
  585.0 8.6 collective-permute-start.17
  610.3 8.6 collective-permute-start.18
  635.6 8.6 collective-permute-start.19
  660.9 8.6 collective-permute-start.20
  686.2 8.6 collective-permute-start.21
  711.5 8.6 collective-permute-start.22
  746.0 3.5 collective-permute-start.23
  758.8 8.6 collective-permute-start.24
  776.6 8.6 collective-permute-start.25
  794.4 8.6 collective-permute-start.26
  812.2 8.6 collective-permute-start.27
  830.0 8.6 collective-permute-start.28
  847.7 8.6 collective-permute-start.29
  865.5 146.3 %copy-start.1 = (f32[8,7,64,64]{3,2,1,0:T(8,128)S(1)}, f32[8,7,64,64]{3,2,1,0:T(8,128)}, u32[]{:S(2)}) copy-start(f32[8,7,64,64]{3,2,1,0:T(8,128)} %param.78) | copy-start | bytes 2752516
  995.6 15.5 %collective-permute-start.30 = (f32[8,512]{1,0:T(8,128)S(1)}, f32[8,512]{1,0:T(8,128)S(1)}, u32[]{:S(2)}, u32[]{:S(2)}) collective-permute-start(f32[8,512]{1,0:T(8,128)S(1)} %convolution_add_fusion.1), channel_id=1, source_target_pairs={{0,8},{8,16},{16,24},{24,32},{32,40},{40,48},{48,56},{56,64},{64,7... | collective-permute-start | bytes 49160 | tf_op jit(solution)/shard_map/ppermute | solution.py:22
  997.5 13.6 %collective-permute-start.31 = (f32[8,512]{1,0:T(8,128)S(1)}, f32[8,512]{1,0:T(8,128)S(1)}, u32[]{:S(2)}, u32[]{:S(2)}) collective-permute-start(f32[8,512]{1,0:T(8,128)S(1)} %convolution_add_fusion.1), channel_id=1, source_target_pairs={{8,0},{16,8},{24,16},{32,24},{40,32},{48,40},{56,48},{64,56},{72,6... | collective-permute-start | bytes 49160 | tf_op jit(solution)/shard_map/ppermute | solution.py:25
  1005.3 34.5 %all-to-all-start.1 = ((f32[8,8,512]{2,1,0:T(8,128)}), f32[8,8,512]{2,1,0:T(8,128)S(1)}, u32[]{:S(2)}, u32[]{:S(2)}) async-start(f32[8,8,512]{2,1,0:T(8,128)} %stack.5), calls=%async_computation.1 | async-start | bytes 262144 | tf_op jit(solution)/shard_map/all_to_all | solution.py:114
